TPU v7x, 512 devices: a whole 4x4x16 slice. The times are simulated.
512 devices in a mesh: space: 16 (over y, x), mom: 32 (over z, core).
Axes of the slice: x: 4, y: 4, z: 16, core: 2. Of those that a mesh axis runs over, the one named last changes fastest.
Arguments:
- distribution: float32 [3, 512, 8, 96, 128], P(None, 'space', None, 'mom'), as said below
- cutoff: int32 [512, 8], P('space'), may hold values from 48 to 96
- phonon_shift: int32 [4], replicated, may hold values from 1 to 8
- phonon_rates: float32 [2, 4], replicated, may hold values from 0.02 to 0.12
Outputs:
- sectioned: float32 [3, 512, 8, 96, 128], P(None, 'space', None, 'mom')
- density: float32 [4096], P(('space', 'mom'))
Inputs may be any that keep to these rules, and one draw needn't show every extreme that they name: `distribution`: the cell means (component 0) are positive.
All inputs are finite; a program needn't handle non-finite values.
Results may differ from a plain program's by a relative error of at most 0.0003.
Values sent between devices are 32-bit elements; how exact they have to be, the bound alone decides.
A program may use at most 64 MiB of HBM per device.

v0:
```python
import math

import jax
import jax.numpy as jnp
from jax import lax
from jax.sharding import PartitionSpec as P

NE = 96
NPOL = 16
NAZ = 8
NDIR = 128


COURANT = 0.25
FLOOR = 0.1


def padded_2(x, sides, width):
    for axis, dim in sides:
        count, length = (lax.axis_size(axis), x.shape[dim])
        up = [(i, (i + 1) % count) for i in range(count - 1)]
        down = [(j, i) for i, j in up]
        last = lax.slice_in_dim(x, length - width, length, axis=dim)
        leading = lax.slice_in_dim(x, 0, width, axis=dim)
        before = lax.ppermute(last, axis, up)
        after = lax.ppermute(leading, axis, down)
        x = jnp.concatenate([before, x, after], axis=dim)
    return x


def velocities(energy):
    flight_speed = jnp.sqrt((energy + 0.5) / NE)
    polar_index = jnp.arange(NPOL, dtype=jnp.float32)
    cos_polar = -1.0 + (2.0 * polar_index + 1.0) / NPOL
    azimuth = (jnp.arange(NAZ, dtype=jnp.float32) + 0.5) * (2.0 * math.pi / NAZ)
    along_x = jnp.repeat(cos_polar, NAZ)
    across_y = (jnp.sqrt(1.0 - cos_polar * cos_polar)[:, None] * jnp.cos(azimuth)[None, :]).reshape(
        NPOL * NAZ
    )
    return (COURANT * flight_speed * along_x, COURANT * flight_speed * across_y)


def transport(padded, vel_x, vel_y):
    level = padded[0]
    slope_x = padded[1]
    slope_y = padded[2]
    right_vel = jnp.maximum(vel_x, 0.0)
    left_vel = jnp.minimum(vel_x, 0.0)
    face_mean = right_vel * (level + slope_x)[:-1] + left_vel * (level - slope_x)[1:]
    face_cross = right_vel * slope_y[:-1] + left_vel * slope_y[1:]
    inner_level = level[1:-1]
    inner_x = slope_x[1:-1]
    inner_y = slope_y[1:-1]
    rate_level = -(face_mean[1:] - face_mean[:-1])
    rate_x = -3.0 * (face_mean[1:] + face_mean[:-1] - 2.0 * vel_x * inner_level)
    rate_y = -(face_cross[1:] - face_cross[:-1])
    widths = [(0, 0)] * inner_level.ndim
    widths[1] = (1, 1)
    pad_level = jnp.pad(inner_level, widths)
    pad_x = jnp.pad(inner_x, widths)
    pad_y = jnp.pad(inner_y, widths)
    up_vel = jnp.maximum(vel_y, 0.0)
    down_vel = jnp.minimum(vel_y, 0.0)
    edge_mean = up_vel * (pad_level + pad_y)[:, :-1] + down_vel * (pad_level - pad_y)[:, 1:]
    edge_cross = up_vel * pad_x[:, :-1] + down_vel * pad_x[:, 1:]
    rate_level = rate_level - (edge_mean[:, 1:] - edge_mean[:, :-1])
    rate_y = rate_y - 3.0 * (edge_mean[:, 1:] + edge_mean[:, :-1] - 2.0 * vel_y * inner_level)
    rate_x = rate_x - (edge_cross[:, 1:] - edge_cross[:, :-1])
    return jnp.stack([rate_level, rate_x, rate_y])


def kernel_parts(phonon_rates, phonon_shift):
    target = jnp.arange(NE, dtype=jnp.int32)[:, None]
    source = jnp.arange(NE, dtype=jnp.int32)[None, :]
    offsets = phonon_shift[:, None, None]
    absorb = (source[None] == target[None] - offsets).astype(jnp.float32)
    emitted = (source[None] == target[None] + offsets).astype(jnp.float32)
    matrix = jnp.sum(
        phonon_rates[0][:, None, None] * absorb + phonon_rates[1][:, None, None] * emitted, axis=0
    )
    energy = jnp.arange(NE, dtype=jnp.int32)[None, :]
    upper = (energy + phonon_shift[:, None] < NE).astype(jnp.float32)
    lower = (energy - phonon_shift[:, None] >= 0).astype(jnp.float32)
    out_rate = jnp.sum(phonon_rates[0][:, None] * upper + phonon_rates[1][:, None] * lower, axis=0)
    return (matrix, out_rate)


def limit(state):
    spread = jnp.abs(state[1]) + jnp.abs(state[2])
    scaling = jnp.minimum(1.0, jnp.maximum(state[0], 0.0) / jnp.maximum(spread, FLOOR))
    return jnp.stack([state[0], scaling * state[1], scaling * state[2]])


def on_device(distribution, cutoff, phonon_shift, phonon_rates):
    comps, slab_x, rows_y, local_e, dirs = distribution.shape
    cells = slab_x * rows_y
    first_energy = lax.axis_index("mom") * local_e
    levels = first_energy + jnp.arange(local_e, dtype=jnp.int32)
    mask = (levels[None, None, :] < cutoff[:, :, None]).astype(jnp.float32)
    masked = distribution * mask[None, :, :, :, None]
    vel_x, vel_y = velocities(levels.astype(jnp.float32)[:, None])
    padded = padded_2(masked, (("space", 1),), 1)
    tendency = transport(padded, vel_x, vel_y)
    matrix, out_rate = kernel_parts(phonon_rates, phonon_shift)
    flat = masked.reshape(comps, cells, local_e, dirs)
    block = lax.all_to_all(flat, "mom", split_axis=1, concat_axis=2, tiled=True)
    angular = jnp.mean(block, axis=3)
    gain = jnp.einsum("dce,fe->dcf", angular, matrix, precision=lax.Precision.HIGHEST)
    scattered = gain[..., None] - out_rate[None, None, :, None] * block
    collision = lax.all_to_all(scattered, "mom", split_axis=2, concat_axis=1, tiled=True).reshape(
        comps, slab_x, rows_y, local_e, dirs
    )
    sectioned = limit(mask[None, :, :, :, None] * (masked + tendency + collision))
    partial_sum = jnp.sum(sectioned[0], axis=(2, 3)).reshape(cells) / (NE * NDIR)
    density = lax.psum_scatter(partial_sum, "mom", scatter_dimension=0, tiled=True)
    return (sectioned, density)


def solution(mesh):
    placed = (P(None, "space", None, "mom", None), P("space", None), P(), P())
    return jax.shard_map(
        on_device,
        mesh=mesh,
        in_specs=placed,
        out_specs=(P(None, "space", None, "mom", None), P(("space", "mom"))),
        check_vma=False,
    )
```

profile of v0, /device:TPU:24, one launch (start us, length us, event | category | flops | bytes accessed | tf_op | source)
XLA Modules:
  0.0 217.5 jit_solution(15695221641093927943)
XLA Ops:
  0.6 0.8 copy.43
  1.4 0.1 compare_convert_fusion
  1.5 0.6 copy-done.3
  2.1 1.4 fusion.28
  3.5 2.0 copy.45
  5.5 15.6 %all-to-all-start = ((f32[3,256,3,128]{3,2,0,1:T(4,128)}), f32[3,256,3,128]{3,2,0,1:T(4,128)S(1)}, u32[]{:S(2)}, u32[]{:S(2)}) async-start(f32[3,256,3,128]{3,2,0,1:T(4,128)} %copy.45), calls=%async_computation | async-start | bytes 3145728 | tf_op jit(solution)/shard_map/all_to_all | solution.py:106
  21.1 0.0 copy-done.5
  21.2 0.1 add_reduce_fusion.1
  21.3 0.1 iota_subtract_fusion
  21.3 0.2 add_reduce_fusion
  21.5 77.8 %all-to-all-done = f32[3,256,3,128]{3,2,0,1:T(4,128)S(1)} async-done(((f32[3,256,3,128]{3,2,0,1:T(4,128)}), f32[3,256,3,128]{3,2,0,1:T(4,128)S(1)}, u32[]{:S(2)}, u32[]{:S(2)}) %all-to-all-start) | async-done | bytes 1179680 | tf_op jit(solution)/shard_map/all_to_all | solution.py:106
  99.3 0.4 fusion.25
  99.7 0.1 copy.51
  99.8 0.1 copy.47
  99.9 0.1 copy.48
  100.0 0.1 div.33
  100.1 0.3 fusion.23
  100.4 0.5 multiply_subtract_fusion
  100.9 1.1 copy.52
  101.9 4.1 %all-to-all-start.1 = ((f32[3,8,96,128]{3,1,0,2:T(8,128)}), f32[3,8,96,128]{3,1,0,2:T(8,128)S(1)}, u32[]{:S(2)}, u32[]{:S(2)}) async-start(f32[3,8,96,128]{3,1,0,2:T(8,128)} %copy.52), calls=%async_computation.1 | async-start | bytes 2359296 | tf_op jit(solution)/shard_map/all_to_all | solution.py:110
  106.0 0.0 copy-done
  106.0 1.0 copy_multiply_fusion
  107.0 0.6 fusion.26
  107.7 4.8 %collective-permute-start.1 = (f32[3,1,8,3,128]{4,2,1,3,0:T(8,128)}, f32[3,1,8,3,128]{4,2,1,3,0:T(8,128)}, u32[]{:S(2)}, u32[]{:S(2)}) collective-permute-start(f32[3,1,8,3,128]{4,2,1,3,0:T(8,128)} %get-tuple-element.27), channel_id=1, source_target_pairs={{32,0},{64,32},{96,64},{128,96},{160,128},{192,160},{224,192},{256... | collective-permute-start | bytes 110600 | tf_op jit(solution)/shard_map/ppermute | solution.py:26
  112.5 1.9 collective-permute-start
  114.5 0.1 broadcast_in_dim.2
  114.5 0.6 mul.271
  115.2 0.1 broadcast_multiply_fusion.2
  115.3 0.7 mul.283
  116.0 0.8 multiply_multiply_fusion.1
  116.7 0.1 slice_bitcast_fusion
  116.8 1.5 fusion.3
  118.3 1.3 dynamic-slice
  120.2 0.0 collective-permute-done.1
  120.2 0.6 collective-permute-done
  120.8 0.8 pad_maximum_fusion.3
  121.6 1.0 fusion.15
  122.6 0.2 copy-done.1
  122.8 0.2 copy-done.2
  123.0 1.3 fusion.22
  124.3 43.9 %all-to-all-done.1 = f32[3,8,96,128]{3,1,0,2:T(8,128)S(1)} async-done(((f32[3,8,96,128]{3,1,0,2:T(8,128)}), f32[3,8,96,128]{3,1,0,2:T(8,128)S(1)}, u32[]{:S(2)}, u32[]{:S(2)}) %all-to-all-start.1) | async-done | bytes 1179680 | tf_op jit(solution)/shard_map/all_to_all | solution.py:110
  168.1 1.5 fusion.1
  169.6 0.2 slice_reduce_fusion
  169.8 0.1 pad_maximum_fusion
  169.9 1.1 copy.55
  171.0 0.1 div.37
  171.1 45.8 %all-reduce.3 = f32[256]{0:T(256)S(1)} all-reduce(f32[256]{0:T(256)S(1)} %div.37), channel_id=2, replica_groups=mesh['space'=16,'mom'=32] {'mom'}, use_global_device_ids=true, to_apply=%region_4.5.clone | all-reduce | flops 256 | bytes 2048
  216.9 0.6 dynamic-slice.1
  (15 shorter events, 0.1 us)
Async XLA Ops:
  1.5 0.6 copy-start.3
  5.5 15.6 %copy-start.5 = (f32[2,4]{1,0:T(2,128)S(1)}, f32[2,4]{1,0:T(2,128)}, u32[]{:S(2)}) copy-start(f32[2,4]{1,0:T(2,128)} %param.7) | copy-start | bytes 100
  5.5 15.6 %copy-start.4 = (s32[4]{0:T(128)S(1)}, s32[4]{0:T(128)}, u32[]{:S(2)}) copy-start(s32[4]{0:T(128)} %param.6) | copy-start | bytes 52
  5.5 93.8 %all-to-all-start = ((f32[3,256,3,128]{3,2,0,1:T(4,128)}), f32[3,256,3,128]{3,2,0,1:T(4,128)S(1)}, u32[]{:S(2)}, u32[]{:S(2)}) async-start(f32[3,256,3,128]{3,2,0,1:T(4,128)} %copy.45), calls=%async_computation | async-start | bytes 3145728 | tf_op jit(solution)/shard_map/all_to_all | solution.py:106
  101.9 4.1 %copy-start = (f32[3,32,8,3,128]{4,2,3,1,0:T(8,128)S(1)}, f32[3,32,8,3,128]{4,2,3,1,0:T(8,128)}, u32[]{:S(2)}) copy-start(f32[3,32,8,3,128]{4,2,3,1,0:T(8,128)} %param.4) | copy-start | bytes 3538948
  101.9 66.2 %all-to-all-start.1 = ((f32[3,8,96,128]{3,1,0,2:T(8,128)}), f32[3,8,96,128]{3,1,0,2:T(8,128)S(1)}, u32[]{:S(2)}, u32[]{:S(2)}) async-start(f32[3,8,96,128]{3,1,0,2:T(8,128)} %copy.52), calls=%async_computation.1 | async-start | bytes 2359296 | tf_op jit(solution)/shard_map/all_to_all | solution.py:110
  107.7 12.5 %collective-permute-start.1 = (f32[3,1,8,3,128]{4,2,1,3,0:T(8,128)}, f32[3,1,8,3,128]{4,2,1,3,0:T(8,128)}, u32[]{:S(2)}, u32[]{:S(2)}) collective-permute-start(f32[3,1,8,3,128]{4,2,1,3,0:T(8,128)} %get-tuple-element.27), channel_id=1, source_target_pairs={{32,0},{64,32},{96,64},{128,96},{160,128},{192,160},{224,192},{256... | collective-permute-start | bytes 110600 | tf_op jit(solution)/shard_map/ppermute | solution.py:26
  112.5 8.3 %collective-permute-start = (f32[3,1,8,3,128]{4,2,1,3,0:T(8,128)}, f32[3,1,8,3,128]{4,2,1,3,0:T(8,128)}, u32[]{:S(2)}, u32[]{:S(2)}) collective-permute-start(f32[3,1,8,3,128]{4,2,1,3,0:T(8,128)} %get-tuple-element.26), channel_id=1, source_target_pairs={{0,32},{32,64},{64,96},{96,128},{128,160},{160,192},{192,224},{224... | collective-permute-start | bytes 110600 | tf_op jit(solution)/shard_map/ppermute | solution.py:25
  121.6 1.2 copy-start.1
  121.6 1.4 copy-start.2
where the time goes:
time: 219 us; the launch traced here: 217 us
  waiting for transfers between devices  122 us (56%)
  blocking collectives  45.8 us (21%)
  starting transfers between devices  26.4 us (12%)
  other arithmetic  10.9 us (5%)
  local copies, waits for them, and re-layouts  10.3 us (5%)
    all_to_all x1, waiting for transfers between devices, on_device(): block = lax.all_to_all(flat, 'mom', split_axis=1, concat_axis=2, tiled=True)  77.8 us
    unnamed x1, blocking collectives  45.8 us
    all_to_all x1, waiting for transfers between devices, on_device(): lax.all_to_all(scattered, 'mom', split_axis=2, concat_axis=1, tiled=True)  43.9 us
    all_to_all x1, starting transfers between devices, on_device(): block = lax.all_to_all(flat, 'mom', split_axis=1, concat_axis=2, tiled=True)  15.6 us
    ppermute x1, starting transfers between devices, padded_2(): after = lax.ppermute(leading, axis, down)  4.83 us
    unnamed x16, local copies, waits for them, and re-layouts  4.73 us
  transfers between devices with their start and end apart: 4, of which 3 were waited for; matrix products, arithmetic and copies ran while one was open for 5% of the time, Pallas kernels for 0%

commit v1 on v0

--- a/solution.py
+++ b/solution.py
@@ -102,14 +102,14 @@
     padded = padded_2(masked, (("space", 1),), 1)
     tendency = transport(padded, vel_x, vel_y)
     matrix, out_rate = kernel_parts(phonon_rates, phonon_shift)
-    flat = masked.reshape(comps, cells, local_e, dirs)
-    block = lax.all_to_all(flat, "mom", split_axis=1, concat_axis=2, tiled=True)
-    angular = jnp.mean(block, axis=3)
-    gain = jnp.einsum("dce,fe->dcf", angular, matrix, precision=lax.Precision.HIGHEST)
-    scattered = gain[..., None] - out_rate[None, None, :, None] * block
-    collision = lax.all_to_all(scattered, "mom", split_axis=2, concat_axis=1, tiled=True).reshape(
-        comps, slab_x, rows_y, local_e, dirs
+    angular = jnp.mean(masked, axis=4).reshape(comps, cells, local_e)
+    block = lax.all_to_all(angular, "mom", split_axis=1, concat_axis=2, tiled=True)
+    gain = jnp.einsum("dce,fe->dcf", block, matrix, precision=lax.Precision.HIGHEST)
+    gain = lax.all_to_all(gain, "mom", split_axis=2, concat_axis=1, tiled=True).reshape(
+        comps, slab_x, rows_y, local_e, 1
     )
+    local_out = lax.dynamic_slice_in_dim(out_rate, first_energy, local_e)
+    collision = gain - local_out[:, None] * masked
     sectioned = limit(mask[None, :, :, :, None] * (masked + tendency + collision))
     partial_sum = jnp.sum(sectioned[0], axis=(2, 3)).reshape(cells) / (NE * NDIR)
     density = lax.psum_scatter(partial_sum, "mom", scatter_dimension=0, tiled=True)

time: 219 us -> 140 us (0.64)
  waiting for transfers between devices: 122 us -> 45.3 us
    all_to_all x2, waiting for transfers between devices: 122 us -> 45.2 us  [the longest x1 26.6 us: on_device(): lax.all_to_all(angular, 'mom', split_axis=1, concat_axis=2, tiled=True)]
    unnamed x16 -> x15, local copies, waits for them, and re-layouts: 4.73 us -> 2.71 us
  transfers between devices with their start and end apart: 4 -> 4, of which waited for: 3 -> 2; matrix products, arithmetic and copies ran while one was open for 5% -> 8% of each run, Pallas kernels for 0% -> 0%
where the time goes in v1:
time: 140 us; the launch traced here: 138 us
  blocking collectives  45.8 us (33%)
  waiting for transfers between devices  45.3 us (32%)
  starting transfers between devices  26.9 us (19%)
  local copies, waits for them, and re-layouts  9.41 us (7%)
  other arithmetic  9.18 us (7%)
  between operations  1.55 us (1%)
    unnamed x1, blocking collectives  45.8 us
    all_to_all x1, waiting for transfers between devices, on_device(): lax.all_to_all(angular, 'mom', split_axis=1, concat_axis=2, tiled=True)  26.6 us
    all_to_all x1, waiting for transfers between devices, on_device(): lax.all_to_all(gain, 'mom', split_axis=2, concat_axis=1, tiled=True)  18.7 us
    all_to_all x1, starting transfers between devices, on_device(): lax.all_to_all(angular, 'mom', split_axis=1, concat_axis=2, tiled=True)  15.5 us
    ppermute x1, starting transfers between devices, padded_2(): after = lax.ppermute(leading, axis, down)  4.83 us
    all_to_all x1, starting transfers between devices, on_device(): lax.all_to_all(gain, 'mom', split_axis=2, concat_axis=1, tiled=True)  4.7 us
  transfers between devices with their start and end apart: 4, of which 2 were waited for; matrix products, arithmetic and copies ran while one was open for 8% of the time, Pallas kernels for 0%

profile of v1, /device:TPU:24, one launch (start us, length us, event | category | flops | bytes accessed | tf_op | source)
XLA Modules:
  0.0 138.5 jit_solution(6967366421722105181)
XLA Ops:
  0.6 0.8 copy.32
  1.4 0.1 compare_convert_fusion
  1.5 1.9 %fusion.25 = (f32[3,32,8,3]{2,3,1,0:T(4,128)S(1)}, f32[3,32,8,3,128]{4,2,3,1,0:T(8,128)S(1)}) fusion(f32[3,32,8,3,128]{4,2,3,1,0:T(8,128)} %param.4, f32[32,8,3]{1,2,0:T(4,128)S(1)} %compare_convert_fusion), kind=kLoop, calls=%fused_computation.73 | loop fusion | flops 587520 | bytes 2371584 | tf_op jit(solution)/shard_map/reduce_sum | solution.py:105
  3.4 0.6 fusion.26
  4.0 4.8 %collective-permute-start.1 = (f32[3,1,8,3,128]{4,2,3,1,0:T(8,128)}, f32[3,1,8,3,128]{4,2,3,1,0:T(8,128)S(1)}, u32[]{:S(2)}, u32[]{:S(2)}) collective-permute-start(f32[3,1,8,3,128]{4,2,3,1,0:T(8,128)} %get-tuple-element.17), channel_id=1, source_target_pairs={{32,0},{64,32},{96,64},{128,96},{160,128},{192,160},{224,192},{256... | collective-permute-start | bytes 110600 | tf_op jit(solution)/shard_map/ppermute | solution.py:26
  8.9 1.9 %collective-permute-start = (f32[3,1,8,3,128]{4,2,3,1,0:T(8,128)}, f32[3,1,8,3,128]{4,2,3,1,0:T(8,128)S(1)}, u32[]{:S(2)}, u32[]{:S(2)}) collective-permute-start(f32[3,1,8,3,128]{4,2,3,1,0:T(8,128)} %get-tuple-element.16), channel_id=1, source_target_pairs={{0,32},{32,64},{64,96},{96,128},{128,160},{160,192},{192,224},{224... | collective-permute-start | bytes 110600 | tf_op jit(solution)/shard_map/ppermute | solution.py:25
  10.8 0.1 copy.33
  10.9 1.3 copy.42
  12.2 15.5 %all-to-all-start = ((f32[3,256,3]{2,0,1:T(4,128)}), f32[3,256,3]{2,0,1:T(4,128)S(1)}, u32[]{:S(2)}, u32[]{:S(2)}) async-start(f32[3,256,3]{2,0,1:T(4,128)} %bitcast.10), calls=%async_computation | async-start | bytes 1048576 | tf_op jit(solution)/shard_map/all_to_all | solution.py:106
  27.6 0.0 copy-start.4
  27.7 0.0 copy-start.3
  27.7 1.1 slice_bitcast_fusion
  28.8 0.1 broadcast_in_dim.2
  28.9 0.1 mul.271
  29.0 0.1 broadcast_multiply_fusion.3
  29.1 0.1 mul.283
  29.2 0.0 copy-done.3
  29.2 0.1 iota_subtract_fusion
  29.3 0.7 multiply_multiply_fusion.1
  29.9 0.2 add_reduce_fusion
  30.1 2.1 %fusion.3 = (f32[32,9,3,128]{3,1,2,0:T(8,128)S(1)}, f32[32,9,3,128]{3,1,2,0:T(8,128)S(1)}) fusion(f32[32,8,3,128]{3,1,2,0:T(8,128)} %get-tuple-element.13, f32[3,128]{1,0:T(4,128)S(1)} %get-tuple-element.33, f32[3,128]{1,0:T(4,128)S(1)} %get-tuple-element.32, f32[32,8,3,128]{3,1,2,0:T(8,128)} %get-tuple-element.14, f32[32,8,3,128]{3,1,2,0:T(8,128)} %get-tuple-element.15), kind=kLoop, calls=%fused_computation.7 | loop fusion | flops 884736 | bytes 2067456 | tf_op jit(solution)/shard_map/add | solution.py:65
  32.2 0.1 add_reduce_fusion.1
  32.3 0.6 dynamic_slice.3
  32.8 1.3 dynamic-slice
  34.9 26.6 %all-to-all-done = f32[3,256,3]{2,0,1:T(4,128)S(1)} async-done(((f32[3,256,3]{2,0,1:T(4,128)}), f32[3,256,3]{2,0,1:T(4,128)S(1)}, u32[]{:S(2)}, u32[]{:S(2)}) %all-to-all-start) | async-done | bytes 9248 | tf_op jit(solution)/shard_map/all_to_all | solution.py:106
  61.4 0.7 copy.43
  62.1 0.1 copy.37
  62.2 0.1 all_to_all.27
  62.3 0.3 fusion.23
  62.7 0.8 copy.39
  63.5 4.7 %all-to-all-start.1 = ((f32[3,8,96]{1,0,2:T(4,128)}), f32[3,8,96]{1,0,2:T(4,128)}, u32[]{:S(2)}, u32[]{:S(2)}) async-start(f32[3,8,96]{1,0,2:T(4,128)} %copy.39), calls=%async_computation.1 | async-start | bytes 393216 | tf_op jit(solution)/shard_map/all_to_all | solution.py:108
  68.2 0.0 collective-permute-done.1
  68.2 0.0 collective-permute-done
  68.2 0.1 pad_maximum_fusion.3
  68.3 0.0 copy-done.1
  68.3 0.0 copy-done.2
  68.3 0.1 fusion.15
  68.4 0.0 copy-start.5
  68.5 1.1 fusion.22
  69.5 18.7 %all-to-all-done.1 = f32[3,8,96]{1,0,2:T(4,128)} async-done(((f32[3,8,96]{1,0,2:T(4,128)}), f32[3,8,96]{1,0,2:T(4,128)}, u32[]{:S(2)}, u32[]{:S(2)}) %all-to-all-start.1) | async-done | bytes 9248 | tf_op jit(solution)/shard_map/all_to_all | solution.py:108
  88.2 1.0 copy.47
  89.2 0.0 copy-done.5
  89.2 1.5 %fusion.1 = f32[3,32,8,3,128]{4,2,3,1,0:T(8,128)S(1)} fusion(f32[3,32,8,3,128]{4,2,3,1,0:T(8,128)S(1)} %get-tuple-element.3, f32[1,32,8,3,128]{4,2,3,1,0:T(8,128)S(1)} %get-tuple-element.11, f32[1,32,8,3,128]{4,2,3,1,0:T(8,128)S(1)} %get-tuple-element.10, f32[1,32,8,3,128]{4,2,3,1,0:T(8,128)} %get-tuple-element.12, f32[3]{0:T(128)S(1)} %copy-done.5, ...), kind=kLoop, calls=%fused_computation.2 | loop fusion | flops 2064384 | bytes 3551244 | tf_op jit(solution)/shard_map/mul | solution.py:113
  90.7 0.2 slice_reduce_fusion
  90.9 0.1 div.37
  91.0 45.8 %all-reduce.3 = f32[256]{0:T(256)S(1)} all-reduce(f32[256]{0:T(256)S(1)} %div.37), channel_id=2, replica_groups=mesh['space'=16,'mom'=32] {'mom'}, use_global_device_ids=true, to_apply=%region_4.5.clone | all-reduce | flops 256 | bytes 2048
  136.8 0.6 dynamic-slice.1
  137.4 1.1 pad_maximum_fusion
  (13 shorter events, 0.1 us)
Async XLA Ops:
  1.5 1.9 %copy-start = (f32[32,8,3]{1,2,0:T(4,128)}, f32[32,8,3]{1,2,0:T(4,128)S(1)}, u32[]{:S(2)}) copy-start(f32[32,8,3]{1,2,0:T(4,128)S(1)} %compare_convert_fusion) | copy-start | bytes 9220
  4.0 64.2 %collective-permute-start.1 = (f32[3,1,8,3,128]{4,2,3,1,0:T(8,128)}, f32[3,1,8,3,128]{4,2,3,1,0:T(8,128)S(1)}, u32[]{:S(2)}, u32[]{:S(2)}) collective-permute-start(f32[3,1,8,3,128]{4,2,3,1,0:T(8,128)} %get-tuple-element.17), channel_id=1, source_target_pairs={{32,0},{64,32},{96,64},{128,96},{160,128},{192,160},{224,192},{256... | collective-permute-start | bytes 110600 | tf_op jit(solution)/shard_map/ppermute | solution.py:26
  8.9 59.4 %collective-permute-start = (f32[3,1,8,3,128]{4,2,3,1,0:T(8,128)}, f32[3,1,8,3,128]{4,2,3,1,0:T(8,128)S(1)}, u32[]{:S(2)}, u32[]{:S(2)}) collective-permute-start(f32[3,1,8,3,128]{4,2,3,1,0:T(8,128)} %get-tuple-element.16), channel_id=1, source_target_pairs={{0,32},{32,64},{64,96},{96,128},{128,160},{160,192},{192,224},{224... | collective-permute-start | bytes 110600 | tf_op jit(solution)/shard_map/ppermute | solution.py:25
  12.2 49.3 %all-to-all-start = ((f32[3,256,3]{2,0,1:T(4,128)}), f32[3,256,3]{2,0,1:T(4,128)S(1)}, u32[]{:S(2)}, u32[]{:S(2)}) async-start(f32[3,256,3]{2,0,1:T(4,128)} %bitcast.10), calls=%async_computation | async-start | bytes 1048576 | tf_op jit(solution)/shard_map/all_to_all | solution.py:106
  27.6 1.5 %copy-start.4 = (f32[2,4]{1,0:T(2,128)S(1)}, f32[2,4]{1,0:T(2,128)}, u32[]{:S(2)}) copy-start(f32[2,4]{1,0:T(2,128)} %param.7) | copy-start | bytes 100
  27.7 1.5 %copy-start.3 = (s32[4]{0:T(128)S(1)}, s32[4]{0:T(128)}, u32[]{:S(2)}) copy-start(s32[4]{0:T(128)} %param.6) | copy-start | bytes 52
  63.5 4.8 %copy-start.1 = (f32[3,128]{1,0:T(4,128)S(1)}, f32[3,128]{1,0:T(4,128)}, u32[]{:S(2)}) copy-start(f32[3,128]{1,0:T(4,128)} %get-tuple-element.25) | copy-start | bytes 4612
  63.5 4.8 %copy-start.2 = (f32[3,128]{1,0:T(4,128)S(1)}, f32[3,128]{1,0:T(4,128)}, u32[]{:S(2)}) copy-start(f32[3,128]{1,0:T(4,128)} %get-tuple-element.26) | copy-start | bytes 4612
  63.5 24.7 %all-to-all-start.1 = ((f32[3,8,96]{1,0,2:T(4,128)}), f32[3,8,96]{1,0,2:T(4,128)}, u32[]{:S(2)}, u32[]{:S(2)}) async-start(f32[3,8,96]{1,0,2:T(4,128)} %copy.39), calls=%async_computation.1 | async-start | bytes 393216 | tf_op jit(solution)/shard_map/all_to_all | solution.py:108
  68.4 20.7 %copy-start.5 = (f32[3]{0:T(128)S(1)}, f32[3]{0:T(128)}, u32[]{:S(2)}) copy-start(f32[3]{0:T(128)} %dynamic_slice.3) | copy-start | bytes 40

commit v2 on v1

v2 whole, which is shorter than its diff:
```python
import functools
import math

import jax
import jax.numpy as jnp
from jax import lax
from jax.experimental import pallas as pl
from jax.experimental.pallas import tpu as pltpu
from jax.sharding import PartitionSpec as P

NE = 96
NPOL = 16
NAZ = 8
NDIR = 128
NPHON = 4
COURANT = 0.25
FLOOR = 0.1
MAX_SHIFT = 8

MESH = pl.DeviceIdType.MESH


def cosines():
    lane = lax.broadcasted_iota(jnp.int32, (8, NDIR), 1)
    polar = (lane >> 3).astype(jnp.float32)
    azimuth = lane & 7
    along = -1.0 + (2.0 * polar + 1.0) / NPOL
    big, small = math.cos(math.pi / 8), math.sin(math.pi / 8)
    outer = (azimuth == 0) | (azimuth == 3) | (azimuth == 4) | (azimuth == 7)
    size = jnp.where(outer, big, small)
    left = (azimuth >= 2) & (azimuth <= 5)
    cos_phi = jnp.where(left, -size, size)
    return along, jnp.sqrt(1.0 - along * along) * cos_phi


def lane_sums(rows):
    ones = jnp.ones((8, rows.shape[1]), jnp.bfloat16)
    high = rows.astype(jnp.bfloat16)
    low = (rows - high.astype(jnp.float32)).astype(jnp.bfloat16)
    dims = (((1,), (1,)), ((), ()))
    return lax.dot_general(ones, high, dims, preferred_element_type=jnp.float32) + lax.dot_general(
        ones, low, dims, preferred_element_type=jnp.float32
    )


def kernel(
    n_space,
    n_mom,
    dist_hbm,
    cut_ref,
    shift_ref,
    rates_ref,
    out_ref,
    dens_ref,
    dist_ref,
    masked,
    cutb,
    moments,
    gains,
    totals,
    dens_send,
    dens_recv,
    load_sem,
    halo_send,
    halo_recv,
    mom_send,
    mom_recv,
    den_send,
    den_recv,
):
    comps, nx, ne, ny, nd = dist_ref.shape
    cells = nx * ny
    reach = -(-MAX_SHIFT // ne)
    space = lax.axis_index("space")
    mom = lax.axis_index("mom")
    has_left = space > 0
    has_right = space < n_space - 1

    loads = [
        pltpu.make_async_copy(dist_hbm.at[c], dist_ref.at[c], load_sem.at[c]) for c in range(comps)
    ]
    for load in loads:
        load.start()

    barrier = pltpu.get_barrier_semaphore()

    @pl.loop(1, n_mom)
    def _(i):
        pl.semaphore_signal(
            barrier, inc=1, device_id={"mom": (mom + i) % n_mom}, device_id_type=MESH
        )

    @pl.when(has_left)
    def _():
        pl.semaphore_signal(barrier, inc=1, device_id={"space": space - 1}, device_id_type=MESH)

    @pl.when(has_right)
    def _():
        pl.semaphore_signal(barrier, inc=1, device_id={"space": space + 1}, device_id_type=MESH)

    first = mom * ne
    cut = cut_ref[...].astype(jnp.float32)
    column = lax.broadcasted_iota(jnp.int32, cut.shape, 1)

    for load in loads:
        load.wait()

    @pl.loop(0, nx)
    def _(x):
        bound = jnp.sum(jnp.where(column == x, cut, 0.0), axis=1, keepdims=True)
        bound = jnp.broadcast_to(bound, (ny, nd))
        cutb[x] = bound
        for e in range(ne):
            mask = jnp.where(bound > (first + e).astype(jnp.float32), 1.0, 0.0)
            for c in range(comps):
                masked[c, x + 1, e] = dist_ref[c, x, e] * mask

    row = lax.broadcasted_iota(jnp.int32, (8, comps * cells), 0)
    packed = jnp.zeros((8, comps * cells), jnp.float32)
    for e in range(ne):
        rows = masked[:, 1 : nx + 1, e].reshape(comps * cells, nd)
        packed = jnp.where(row == e, lane_sums(rows) * (1.0 / NDIR), packed)
    moments[reach] = packed

    @pl.when(jnp.logical_not(has_left))
    def _():
        masked[:, 0] = jnp.zeros((comps, ne, ny, nd), jnp.float32)

    @pl.when(jnp.logical_not(has_right))
    def _():
        masked[:, nx + 1] = jnp.zeros((comps, ne, ny, nd), jnp.float32)

    peers = n_mom - 1 + has_left.astype(jnp.int32) + has_right.astype(jnp.int32)
    pl.semaphore_wait(barrier, peers)

    to_left = pltpu.make_async_remote_copy(
        src_ref=masked.at[:, 1],
        dst_ref=masked.at[:, nx + 1],
        send_sem=halo_send.at[0],
        recv_sem=halo_recv.at[0],
        device_id={"space": space - 1},
        device_id_type=MESH,
    )
    to_right = pltpu.make_async_remote_copy(
        src_ref=masked.at[:, nx],
        dst_ref=masked.at[:, 0],
        send_sem=halo_send.at[1],
        recv_sem=halo_recv.at[1],
        device_id={"space": space + 1},
        device_id_type=MESH,
    )

    @pl.when(has_left)
    def _():
        to_left.start()

    @pl.when(has_right)
    def _():
        to_right.start()

    def moment_copy(offset):
        slot = reach - offset
        return pltpu.make_async_remote_copy(
            src_ref=moments.at[reach],
            dst_ref=moments.at[slot],
            send_sem=mom_send.at[slot],
            recv_sem=mom_recv.at[slot],
            device_id={"mom": mom + offset},
            device_id_type=MESH,
        )

    offsets = [o for o in range(-reach, reach + 1) if o != 0]
    for offset in offsets:
        there = (mom + offset >= 0) & (mom + offset < n_mom)

        @pl.when(there)
        def _(offset=offset):
            moment_copy(offset).start()

        @pl.when(jnp.logical_not(there))
        def _(offset=offset):
            moments[reach + offset] = jnp.zeros((8, comps * cells), jnp.float32)

    along, across = cosines()
    depth = (2 * reach + 1) * 8
    k = lax.broadcasted_iota(jnp.int32, (depth, nd), 0)
    source = (mom - reach + (k >> 3)) * ne + (k & 7)
    source = jnp.where((k & 7) < ne, source, -1000)
    weights = []
    keep = []
    speeds = []
    for e in range(ne):
        level = first + e
        weight = jnp.zeros((depth, nd), jnp.float32)
        out_rate = jnp.zeros((ny, nd), jnp.float32)
        for mode in range(NPHON):
            shift = shift_ref[mode]
            weight = weight + jnp.where(source == level - shift, rates_ref[0, mode], 0.0)
            weight = weight + jnp.where(source == level + shift, rates_ref[1, mode], 0.0)
            upper = jnp.full((ny, nd), level + shift, jnp.int32) < NE
            lower = jnp.full((ny, nd), level - shift, jnp.int32) >= 0
            out_rate = out_rate + jnp.where(upper, rates_ref[0, mode], 0.0)
            out_rate = out_rate + jnp.where(lower, rates_ref[1, mode], 0.0)
        weights.append(weight)
        keep.append(1.0 - out_rate)
        energy = jnp.full((ny, nd), level, jnp.int32).astype(jnp.float32)
        speeds.append(COURANT * jnp.sqrt((energy + 0.5) / NE))
    weights = jnp.concatenate(weights, axis=1)

    for offset in offsets:
        there = (mom + offset >= 0) & (mom + offset < n_mom)

        @pl.when(there)
        def _(offset=offset):
            moment_copy(-offset).wait_recv()

    gathered = moments[...].reshape(depth, comps * cells)
    gains[...] = lax.dot_general(
        gathered,
        weights,
        (((0,), (0,)), ((), ())),
        precision=lax.Precision.HIGHEST,
        preferred_element_type=jnp.float32,
    ).reshape(comps, nx, ny, ne * nd)

    @pl.when(has_right)
    def _():
        to_left.wait_recv()

    @pl.when(has_left)
    def _():
        to_right.wait_recv()

    y = lax.broadcasted_iota(jnp.int32, (ny, nd), 0)
    not_first = jnp.where(y > 0, 1.0, 0.0)
    not_last = jnp.where(y < ny - 1, 1.0, 0.0)

    @pl.loop(0, nx)
    def _(x):
        bound = cutb[x]
        total = jnp.zeros((ny, nd), jnp.float32)
        for e in range(ne):
            vx = speeds[e] * along
            vy = speeds[e] * across
            vp, vn = jnp.maximum(vx, 0.0), jnp.minimum(vx, 0.0)
            wp, wn = jnp.maximum(vy, 0.0), jnp.minimum(vy, 0.0)
            wp_below, wn_above = wp * not_first, wn * not_last
            m, gx, gy = masked[0, x + 1, e], masked[1, x + 1, e], masked[2, x + 1, e]
            left_x = masked[0, x, e] + masked[1, x, e]
            right_x = masked[0, x + 2, e] - masked[1, x + 2, e]
            f_right = vp * (m + gx) + vn * right_x
            f_left = vp * left_x + vn * (m - gx)
            h_right = vp * gy + vn * masked[2, x + 2, e]
            h_left = vp * masked[2, x, e] + vn * gy
            up, down = m + gy, m - gy
            p_above = wp * up + wn_above * pltpu.roll(down, ny - 1, 0)
            p_below = wp_below * pltpu.roll(up, 1, 0) + wn * down
            q_above = wp * gx + wn_above * pltpu.roll(gx, ny - 1, 0)
            q_below = wp_below * pltpu.roll(gx, 1, 0) + wn * gx
            mask = jnp.where(bound > (first + e).astype(jnp.float32), 1.0, 0.0)
            lanes = pl.ds(e * nd, nd)
            raw0 = keep[e] * m + gains[0, x, :, lanes] - (f_right - f_left) - (p_above - p_below)
            raw1 = (
                keep[e] * gx
                + gains[1, x, :, lanes]
                - 3.0 * (f_right + f_left - 2.0 * vx * m)
                - (q_above - q_below)
            )
            raw2 = (
                keep[e] * gy
                + gains[2, x, :, lanes]
                - (h_right - h_left)
                - 3.0 * (p_above + p_below - 2.0 * vy * m)
            )
            raw0, raw1, raw2 = mask * raw0, mask * raw1, mask * raw2
            spread = jnp.abs(raw1) + jnp.abs(raw2)
            scaling = jnp.minimum(1.0, jnp.maximum(raw0, 0.0) / jnp.maximum(spread, FLOOR))
            out_ref[0, x, e] = raw0
            out_ref[1, x, e] = scaling * raw1
            out_ref[2, x, e] = scaling * raw2
            total = total + raw0
        totals[x] = total

    flat = lane_sums(totals[...].reshape(cells, nd))[0:1] * (1.0 / (NE * NDIR))
    cell = lax.broadcasted_iota(jnp.int32, (nx, cells), 1)
    column_of = lax.broadcasted_iota(jnp.int32, (nx, cells), 0)
    spread_rows = jnp.where((cell // ny) == column_of, flat, 0.0)
    source_y = lax.broadcasted_iota(jnp.int32, (cells, nd), 0) % ny
    target_y = lax.broadcasted_iota(jnp.int32, (cells, nd), 1)
    pick = jnp.where(source_y == target_y, 1.0, 0.0)
    table = jnp.dot(
        spread_rows, pick, precision=lax.Precision.HIGHEST, preferred_element_type=jnp.float32
    )
    for x in range(nx):
        dens_send[x] = table[x : x + 1]

    def density_copy(target, slot):
        return pltpu.make_async_remote_copy(
            src_ref=dens_send.at[target],
            dst_ref=dens_recv.at[slot],
            send_sem=den_send.at[target],
            recv_sem=den_recv.at[slot],
            device_id={"mom": target},
            device_id_type=MESH,
        )

    @pl.loop(1, n_mom)
    def _(i):
        density_copy((mom + i) % n_mom, mom).start()

    @pl.loop(1, n_mom)
    def _(i):
        other = (mom + i) % n_mom
        density_copy(other, other).wait()

    dens_recv[mom] = dens_send[mom]
    dens_ref[...] = jnp.sum(dens_recv[...], axis=0)[:, :ny]

    for offset in offsets:
        there = (mom + offset >= 0) & (mom + offset < n_mom)

        @pl.when(there)
        def _(offset=offset):
            moment_copy(offset).wait_send()

    @pl.when(has_left)
    def _():
        to_left.wait_send()

    @pl.when(has_right)
    def _():
        to_right.wait_send()


def on_device(n_space, n_mom, distribution, cutoff, phonon_shift, phonon_rates):
    comps, nx, ny, ne, nd = distribution.shape
    reach = -(-MAX_SHIFT // ne)
    by_energy = jnp.transpose(distribution, (0, 1, 3, 2, 4))
    sectioned, density = pl.pallas_call(
        functools.partial(kernel, n_space, n_mom),
        out_shape=(
            jax.ShapeDtypeStruct((comps, nx, ne, ny, nd), jnp.float32),
            jax.ShapeDtypeStruct((1, ny), jnp.float32),
        ),
        in_specs=[
            pl.BlockSpec(memory_space=pl.ANY),
            pl.BlockSpec(memory_space=pltpu.VMEM),
            pl.BlockSpec(memory_space=pltpu.SMEM),
            pl.BlockSpec(memory_space=pltpu.SMEM),
        ],
        out_specs=(
            pl.BlockSpec(memory_space=pltpu.VMEM),
            pl.BlockSpec(memory_space=pltpu.VMEM),
        ),
        scratch_shapes=[
            pltpu.VMEM((comps, nx, ne, ny, nd), jnp.float32),
            pltpu.VMEM((comps, nx + 2, ne, ny, nd), jnp.float32),
            pltpu.VMEM((nx, ny, nd), jnp.float32),
            pltpu.VMEM((2 * reach + 1, 8, comps * nx * ny), jnp.float32),
            pltpu.VMEM((comps, nx, ny, ne * nd), jnp.float32),
            pltpu.VMEM((nx, ny, nd), jnp.float32),
            pltpu.VMEM((n_mom, 1, nd), jnp.float32),
            pltpu.VMEM((n_mom, 1, nd), jnp.float32),
            pltpu.SemaphoreType.DMA((comps,)),
            pltpu.SemaphoreType.DMA((2,)),
            pltpu.SemaphoreType.DMA((2,)),
            pltpu.SemaphoreType.DMA((2 * reach + 1,)),
            pltpu.SemaphoreType.DMA((2 * reach + 1,)),
            pltpu.SemaphoreType.DMA((n_mom,)),
            pltpu.SemaphoreType.DMA((n_mom,)),
        ],
        compiler_params=pltpu.CompilerParams(collective_id=0, has_side_effects=True),
        name="section",
    )(by_energy, jnp.transpose(cutoff), phonon_shift, phonon_rates)
    return jnp.transpose(sectioned, (0, 1, 3, 2, 4)), density.reshape(ny)


def solution(mesh):
    return jax.shard_map(
        functools.partial(on_device, mesh.shape["space"], mesh.shape["mom"]),
        mesh=mesh,
        in_specs=(P(None, "space", None, "mom", None), P("space", None), P(), P()),
        out_specs=(P(None, "space", None, "mom", None), P(("space", "mom"))),
        check_vma=False,
    )
```

time: 140 us -> 36 us (0.26)
  the two profiles are of different devices: /device:TPU:24 before, /device:TPU:1 now
where the time goes in v2:
time: 36 us; the launch traced here: 35.8 us
  Pallas kernels  32.3 us (90%)
  local copies, waits for them, and re-layouts  2.88 us (8%)
  between operations  0.65 us (2%)
    pallas_call x1, Pallas kernels, on_device(): pl.pallas_call(functools.partial(kernel, n_space, n_mom), out_shape=(jax....  32.3 us
    unnamed x4, local copies, waits for them, and re-layouts  2.88 us

profile of v2, /device:TPU:1, one launch (start us, length us, event | category | flops | bytes accessed | tf_op | source)
XLA Modules:
  0.0 35.8 jit_solution(994843926775307948)
XLA Ops:
  0.6 32.3 %section.1 = (f32[3,32,3,8,128]{4,3,2,1,0:T(8,128)}, f32[1,8]{1,0:T(1,128)}) custom-call(f32[3,32,3,8,128]{4,3,2,1,0:T(8,128)} %bitcast.4, s32[8,32]{1,0:T(8,128)} %bitcast.6, s32[4]{0:T(128)} %shift_ref.1, f32[2,4]{1,0:T(2,128)} %rates_ref.1), custom_call_target="tpu_custom_call" | custom-call | tf_op jit(solution)/shard_map/section/pallas_call | solution.py:339
  33.0 0.0 copy-start
  33.0 2.4 %copy.8 = f32[3,32,8,3,128]{4,2,3,1,0:T(8,128)} copy(f32[3,32,8,3,128]{4,2,3,1,0:T(8,128)} %bitcast.5) | data formatting | bytes 2359296
  35.3 0.0 copy-done
  35.3 0.5 %copy.9 = f32[8]{0:T(128)} copy(f32[8]{0:T(128)S(1)} %bitcast.7) | data formatting | bytes 64
Async XLA Ops:
  33.0 2.4 %copy-start = (f32[1,8]{1,0:T(1,128)S(1)}, f32[1,8]{1,0:T(1,128)}, u32[]{:S(2)}) copy-start(f32[1,8]{1,0:T(1,128)} %get-tuple-element.5) | copy-start | bytes 100

commit v3 on v2

--- a/solution.py
+++ b/solution.py
@@ -100,16 +100,15 @@
 
     first = mom * ne
     cut = cut_ref[...].astype(jnp.float32)
-    column = lax.broadcasted_iota(jnp.int32, cut.shape, 1)
+    for x in range(nx):
+        cutb[x] = jnp.broadcast_to(cut[:, x : x + 1], (ny, nd))
 
     for load in loads:
         load.wait()
 
-    @pl.loop(0, nx)
+    @pl.loop(0, nx, unroll=4)
     def _(x):
-        bound = jnp.sum(jnp.where(column == x, cut, 0.0), axis=1, keepdims=True)
-        bound = jnp.broadcast_to(bound, (ny, nd))
-        cutb[x] = bound
+        bound = cutb[x]
         for e in range(ne):
             mask = jnp.where(bound > (first + e).astype(jnp.float32), 1.0, 0.0)
             for c in range(comps):
@@ -207,6 +206,53 @@
         speeds.append(COURANT * jnp.sqrt((energy + 0.5) / NE))
     weights = jnp.concatenate(weights, axis=1)
 
+    y = lax.broadcasted_iota(jnp.int32, (ny, nd), 0)
+    from_left = along > 0.0
+    from_below = across > 0.0
+    inside = jnp.where(from_below, jnp.where(y > 0, 1.0, 0.0), jnp.where(y < ny - 1, 1.0, 0.0))
+
+    def upwind(values):
+        return jnp.where(from_below, pltpu.roll(values, 1, 0), pltpu.roll(values, ny - 1, 0))
+
+    def sources(x, e):
+        before = masked[0, x, e] + masked[1, x, e]
+        after = masked[0, x + 2, e] - masked[1, x + 2, e]
+        m, gy = masked[0, x + 1, e], masked[2, x + 1, e]
+        side_x = jnp.where(from_left, before, after)
+        side_y = jnp.where(
+            from_below, pltpu.roll(m + gy, 1, 0), pltpu.roll(m - gy, ny - 1, 0)
+        )
+        return side_x, side_y
+
+    def mask_of(x, e):
+        return jnp.where(cutb[x] > (first + e).astype(jnp.float32), 1.0, 0.0)
+
+    def level_step(x):
+        for e in range(ne):
+            vx, vy = speeds[e] * along, speeds[e] * across
+            ax, ay = jnp.abs(vx), jnp.abs(vy)
+            side_x, side_y = sources(x, e)
+            out_ref[0, x, e] = (
+                (keep[e] - ax - ay) * masked[0, x + 1, e]
+                - vx * masked[1, x + 1, e]
+                - vy * masked[2, x + 1, e]
+                + ax * side_x
+                + ay * inside * side_y
+            )
+
+    pl.loop(1, nx - 1, unroll=3)(level_step)
+
+    @pl.when(has_right)
+    def _():
+        to_left.wait_recv()
+
+    @pl.when(has_left)
+    def _():
+        to_right.wait_recv()
+
+    level_step(0)
+    level_step(nx - 1)
+
     for offset in offsets:
         there = (mom + offset >= 0) & (mom + offset < n_mom)
 
@@ -214,70 +260,24 @@
         def _(offset=offset):
             moment_copy(-offset).wait_recv()
 
-    gathered = moments[...].reshape(depth, comps * cells)
-    gains[...] = lax.dot_general(
-        gathered,
-        weights,
-        (((0,), (0,)), ((), ())),
-        precision=lax.Precision.HIGHEST,
-        preferred_element_type=jnp.float32,
-    ).reshape(comps, nx, ny, ne * nd)
-
-    @pl.when(has_right)
-    def _():
-        to_left.wait_recv()
-
-    @pl.when(has_left)
-    def _():
-        to_right.wait_recv()
-
-    y = lax.broadcasted_iota(jnp.int32, (ny, nd), 0)
-    not_first = jnp.where(y > 0, 1.0, 0.0)
-    not_last = jnp.where(y < ny - 1, 1.0, 0.0)
-
-    @pl.loop(0, nx)
+    def set_gains(c):
+        gathered = moments[:, :, c * cells : (c + 1) * cells].reshape(depth, cells)
+        gains[c] = lax.dot_general(
+            gathered,
+            weights,
+            (((0,), (0,)), ((), ())),
+            precision=lax.Precision.HIGHEST,
+            preferred_element_type=jnp.float32,
+        ).reshape(nx, ny, ne * nd)
+
+    set_gains(0)
+
+    @pl.loop(0, nx, unroll=4)
     def _(x):
-        bound = cutb[x]
         total = jnp.zeros((ny, nd), jnp.float32)
         for e in range(ne):
-            vx = speeds[e] * along
-            vy = speeds[e] * across
-            vp, vn = jnp.maximum(vx, 0.0), jnp.minimum(vx, 0.0)
-            wp, wn = jnp.maximum(vy, 0.0), jnp.minimum(vy, 0.0)
-            wp_below, wn_above = wp * not_first, wn * not_last
-            m, gx, gy = masked[0, x + 1, e], masked[1, x + 1, e], masked[2, x + 1, e]
-            left_x = masked[0, x, e] + masked[1, x, e]
-            right_x = masked[0, x + 2, e] - masked[1, x + 2, e]
-            f_right = vp * (m + gx) + vn * right_x
-            f_left = vp * left_x + vn * (m - gx)
-            h_right = vp * gy + vn * masked[2, x + 2, e]
-            h_left = vp * masked[2, x, e] + vn * gy
-            up, down = m + gy, m - gy
-            p_above = wp * up + wn_above * pltpu.roll(down, ny - 1, 0)
-            p_below = wp_below * pltpu.roll(up, 1, 0) + wn * down
-            q_above = wp * gx + wn_above * pltpu.roll(gx, ny - 1, 0)
-            q_below = wp_below * pltpu.roll(gx, 1, 0) + wn * gx
-            mask = jnp.where(bound > (first + e).astype(jnp.float32), 1.0, 0.0)
-            lanes = pl.ds(e * nd, nd)
-            raw0 = keep[e] * m + gains[0, x, :, lanes] - (f_right - f_left) - (p_above - p_below)
-            raw1 = (
-                keep[e] * gx
-                + gains[1, x, :, lanes]
-                - 3.0 * (f_right + f_left - 2.0 * vx * m)
-                - (q_above - q_below)
-            )
-            raw2 = (
-                keep[e] * gy
-                + gains[2, x, :, lanes]
-                - (h_right - h_left)
-                - 3.0 * (p_above + p_below - 2.0 * vy * m)
-            )
-            raw0, raw1, raw2 = mask * raw0, mask * raw1, mask * raw2
-            spread = jnp.abs(raw1) + jnp.abs(raw2)
-            scaling = jnp.minimum(1.0, jnp.maximum(raw0, 0.0) / jnp.maximum(spread, FLOOR))
+            raw0 = mask_of(x, e) * (out_ref[0, x, e] + gains[0, x, :, e * nd : (e + 1) * nd])
             out_ref[0, x, e] = raw0
-            out_ref[1, x, e] = scaling * raw1
-            out_ref[2, x, e] = scaling * raw2
             total = total + raw0
         totals[x] = total
 
@@ -308,6 +308,37 @@
     def _(i):
         density_copy((mom + i) % n_mom, mom).start()
 
+    for c in range(1, comps):
+        set_gains(c)
+
+    @pl.loop(0, nx, unroll=2)
+    def _(x):
+        for e in range(ne):
+            vx, vy = speeds[e] * along, speeds[e] * across
+            ax, ay = jnp.abs(vx), jnp.abs(vy)
+            side_x, side_y = sources(x, e)
+            m, gx, gy = masked[0, x + 1, e], masked[1, x + 1, e], masked[2, x + 1, e]
+            gy_side = jnp.where(from_left, masked[2, x, e], masked[2, x + 2, e])
+            mask = mask_of(x, e)
+            raw1 = (
+                (keep[e] - 3.0 * ax - ay) * gx
+                + 3.0 * vx * (m - side_x)
+                + ay * inside * upwind(gx)
+                + gains[1, x, :, e * nd : (e + 1) * nd]
+            )
+            raw2 = (
+                (keep[e] - ax - 3.0 * ay) * gy
+                + ax * gy_side
+                + 3.0 * vy * (m - inside * side_y)
+                + gains[2, x, :, e * nd : (e + 1) * nd]
+            )
+            raw1, raw2 = mask * raw1, mask * raw2
+            spread = jnp.abs(raw1) + jnp.abs(raw2)
+            raw0 = out_ref[0, x, e]
+            scaling = jnp.minimum(1.0, jnp.maximum(raw0, 0.0) / jnp.maximum(spread, FLOOR))
+            out_ref[1, x, e] = scaling * raw1
+            out_ref[2, x, e] = scaling * raw2
+
     @pl.loop(1, n_mom)
     def _(i):
         other = (mom + i) % n_mom
@@ -339,8 +370,8 @@
     sectioned, density = pl.pallas_call(
         functools.partial(kernel, n_space, n_mom),
         out_shape=(
-            jax.ShapeDtypeStruct((comps, nx, ne, ny, nd), jnp.float32),
-            jax.ShapeDtypeStruct((1, ny), jnp.float32),
+            pltpu.VMEM((comps, nx, ne, ny, nd), jnp.float32),
+            pltpu.VMEM((1, ny), jnp.float32),
         ),
         in_specs=[
             pl.BlockSpec(memory_space=pl.ANY),

time: 36 us -> 31.4 us (0.87)
  Pallas kernels: 32.3 us -> 29.1 us
  local copies, waits for them, and re-layouts: 2.88 us -> 1.53 us
    pallas_call x1, Pallas kernels: 32.3 us -> 29.1 us  [on_device(): pl.pallas_call(functools.partial(kernel, n_space, n_mom), out_shape=(pltp...]
    unnamed x4 -> x2, local copies, waits for them, and re-layouts: 2.88 us -> 1.53 us
where the time goes in v3:
time: 31.4 us; the launch traced here: 31.3 us
  Pallas kernels  29.1 us (93%)
  local copies, waits for them, and re-layouts  1.53 us (5%)
  between operations  0.64 us (2%)
    pallas_call x1, Pallas kernels, on_device(): pl.pallas_call(functools.partial(kernel, n_space, n_mom), out_shape=(pltp...  29.1 us
    unnamed x2, local copies, waits for them, and re-layouts  1.53 us

profile of v3, /device:TPU:1, one launch (start us, length us, event | category | flops | bytes accessed | tf_op | source)
XLA Modules:
  0.0 31.3 jit_solution(3476850751531018297)
XLA Ops:
  0.6 29.1 %section.1 = (f32[3,32,3,8,128]{4,3,2,1,0:T(8,128)S(1)}, f32[1,8]{1,0:T(1,128)S(1)}) custom-call(f32[3,32,3,8,128]{4,3,2,1,0:T(8,128)} %bitcast.6, s32[8,32]{1,0:T(8,128)} %bitcast.7, s32[4]{0:T(128)} %shift_ref.1, f32[2,4]{1,0:T(2,128)} %rates_ref.1), custom_call_target="tpu_custom_call" | custom-call | tf_op jit(solution)/shard_map/section/pallas_call | solution.py:370
  29.7 1.0 %copy.8 = f32[3,32,8,3,128]{4,2,3,1,0:T(8,128)} copy(f32[3,32,8,3,128]{4,2,3,1,0:T(8,128)S(1)} %bitcast.4) | data formatting | bytes 2359296
  30.8 0.5 %copy.9 = f32[8]{0:T(128)} copy(f32[8]{0:T(128)S(1)} %bitcast.5) | data formatting | bytes 64

commit v4 on v3

--- a/solution.py
+++ b/solution.py
@@ -41,6 +41,11 @@
     return lax.dot_general(ones, high, dims, preferred_element_type=jnp.float32) + lax.dot_general(
         ones, low, dims, preferred_element_type=jnp.float32
     )
+
+
+def parts(values):
+    high = values.astype(jnp.bfloat16).astype(jnp.float32)
+    return high, values - high
 
 
 def kernel(
@@ -121,6 +126,124 @@
         packed = jnp.where(row == e, lane_sums(rows) * (1.0 / NDIR), packed)
     moments[reach] = packed
 
+    along, across = cosines()
+    depth = (2 * reach + 1) * 8
+    k = lax.broadcasted_iota(jnp.int32, (depth, nd), 0)
+    source = (mom - reach + (k >> 3)) * ne + (k & 7)
+    source = jnp.where((k & 7) < ne, source, -1000)
+    weights = []
+    keep = []
+    speeds = []
+    reached = []
+    for e in range(ne):
+        level = first + e
+        weight = jnp.zeros((depth, nd), jnp.float32)
+        out_rate = jnp.zeros((ny, nd), jnp.float32)
+        for mode in range(NPHON):
+            shift = shift_ref[mode]
+            weight = weight + jnp.where(source == level - shift, rates_ref[0, mode], 0.0)
+            weight = weight + jnp.where(source == level + shift, rates_ref[1, mode], 0.0)
+            upper = jnp.full((ny, nd), level + shift, jnp.int32) < NE
+            lower = jnp.full((ny, nd), level - shift, jnp.int32) >= 0
+            out_rate = out_rate + jnp.where(upper, rates_ref[0, mode], 0.0)
+            out_rate = out_rate + jnp.where(lower, rates_ref[1, mode], 0.0)
+        reached.append(
+            [
+                (
+                    jnp.full((ny, nd), level + shift_ref[mode], jnp.int32).astype(jnp.float32),
+                    jnp.full((ny, nd), level - shift_ref[mode], jnp.int32).astype(jnp.float32),
+                    rates_ref[0, mode],
+                    jnp.where(
+                        jnp.full((ny, nd), level - shift_ref[mode], jnp.int32) >= 0,
+                        rates_ref[1, mode],
+                        0.0,
+                    ),
+                )
+                for mode in range(NPHON)
+            ]
+        )
+        weights.append(weight)
+        keep.append(1.0 - out_rate)
+        energy = jnp.full((ny, nd), level, jnp.int32).astype(jnp.float32)
+        speeds.append(COURANT * jnp.sqrt((energy + 0.5) / NE))
+    weights = jnp.concatenate(weights, axis=1)
+    weights_high, weights_low = parts(weights)
+    blank = jnp.zeros((8, ne * nd), jnp.float32)
+    weights = jnp.concatenate([weights_high, weights_high, weights_low, blank], axis=0)
+    weights = weights.astype(jnp.bfloat16)
+
+    y = lax.broadcasted_iota(jnp.int32, (ny, nd), 0)
+    from_left = along > 0.0
+    from_below = across > 0.0
+    inside = jnp.where(from_below, jnp.where(y > 0, 1.0, 0.0), jnp.where(y < ny - 1, 1.0, 0.0))
+
+    def upwind(values):
+        return jnp.where(from_below, pltpu.roll(values, 1, 0), pltpu.roll(values, ny - 1, 0))
+
+    def sources(x, e):
+        before = masked[0, x, e] + masked[1, x, e]
+        after = masked[0, x + 2, e] - masked[1, x + 2, e]
+        m, gy = masked[0, x + 1, e], masked[2, x + 1, e]
+        side_x = jnp.where(from_left, before, after)
+        side_y = jnp.where(
+            from_below, pltpu.roll(m + gy, 1, 0), pltpu.roll(m - gy, ny - 1, 0)
+        )
+        return side_x, side_y
+
+    def mask_of(x, e):
+        return jnp.where(cutb[x] > (first + e).astype(jnp.float32), 1.0, 0.0)
+
+    def level_step(x):
+        bound = jnp.minimum(cutb[x], float(NE))
+        total = jnp.zeros((ny, nd), jnp.float32)
+        for e in range(ne):
+            vx, vy = speeds[e] * along, speeds[e] * across
+            ax, ay = jnp.abs(vx), jnp.abs(vy)
+            side_x, side_y = sources(x, e)
+            level = (
+                (keep[e] - ax - ay) * masked[0, x + 1, e]
+                - vx * masked[1, x + 1, e]
+                - vy * masked[2, x + 1, e]
+                + ax * side_x
+                + ay * inside * side_y
+            )
+            out_ref[0, x, e] = level
+            total = total + mask_of(x, e) * level
+            into = jnp.zeros((ny, nd), jnp.float32)
+            for mode in range(NPHON):
+                above, below, absorb, emit = reached[e][mode]
+                into = into + jnp.where(bound > above, absorb, 0.0)
+                into = into + jnp.where(bound > below, emit, 0.0)
+            total = total + into * masked[0, x + 1, e]
+        totals[x] = total
+
+    totals[0] = jnp.zeros((ny, nd), jnp.float32)
+    totals[nx - 1] = jnp.zeros((ny, nd), jnp.float32)
+    pl.loop(1, nx - 1, unroll=3)(level_step)
+
+    flat = lane_sums(totals[...].reshape(cells, nd))[0:1] * (1.0 / (NE * NDIR))
+    cell = lax.broadcasted_iota(jnp.int32, (nx, cells), 1)
+    column_of = lax.broadcasted_iota(jnp.int32, (nx, cells), 0)
+    spread_rows = jnp.where((cell // ny) == column_of, flat, 0.0)
+    source_y = lax.broadcasted_iota(jnp.int32, (cells, nd), 0) % ny
+    target_y = lax.broadcasted_iota(jnp.int32, (cells, nd), 1)
+    pick = jnp.where(source_y == target_y, 1.0, 0.0)
+    table = jnp.dot(
+        spread_rows, pick, precision=lax.Precision.HIGHEST, preferred_element_type=jnp.float32
+    )
+    for x in range(1, nx - 1):
+        dens_send[x] = table[x : x + 1]
+
+    def density_copy(target, slot):
+        return pltpu.make_async_remote_copy(
+            src_ref=dens_send.at[target],
+            dst_ref=dens_recv.at[slot],
+            send_sem=den_send.at[target],
+            recv_sem=den_recv.at[slot],
+            device_id={"mom": target},
+            device_id_type=MESH,
+        )
+
     @pl.when(jnp.logical_not(has_left))
     def _():
         masked[:, 0] = jnp.zeros((comps, ne, ny, nd), jnp.float32)
@@ -180,67 +303,13 @@
         def _(offset=offset):
             moments[reach + offset] = jnp.zeros((8, comps * cells), jnp.float32)
 
-    along, across = cosines()
-    depth = (2 * reach + 1) * 8
-    k = lax.broadcasted_iota(jnp.int32, (depth, nd), 0)
-    source = (mom - reach + (k >> 3)) * ne + (k & 7)
-    source = jnp.where((k & 7) < ne, source, -1000)
-    weights = []
-    keep = []
-    speeds = []
-    for e in range(ne):
-        level = first + e
-        weight = jnp.zeros((depth, nd), jnp.float32)
-        out_rate = jnp.zeros((ny, nd), jnp.float32)
-        for mode in range(NPHON):
-            shift = shift_ref[mode]
-            weight = weight + jnp.where(source == level - shift, rates_ref[0, mode], 0.0)
-            weight = weight + jnp.where(source == level + shift, rates_ref[1, mode], 0.0)
-            upper = jnp.full((ny, nd), level + shift, jnp.int32) < NE
-            lower = jnp.full((ny, nd), level - shift, jnp.int32) >= 0
-            out_rate = out_rate + jnp.where(upper, rates_ref[0, mode], 0.0)
-            out_rate = out_rate + jnp.where(lower, rates_ref[1, mode], 0.0)
-        weights.append(weight)
-        keep.append(1.0 - out_rate)
-        energy = jnp.full((ny, nd), level, jnp.int32).astype(jnp.float32)
-        speeds.append(COURANT * jnp.sqrt((energy + 0.5) / NE))
-    weights = jnp.concatenate(weights, axis=1)
-
-    y = lax.broadcasted_iota(jnp.int32, (ny, nd), 0)
-    from_left = along > 0.0
-    from_below = across > 0.0
-    inside = jnp.where(from_below, jnp.where(y > 0, 1.0, 0.0), jnp.where(y < ny - 1, 1.0, 0.0))
-
-    def upwind(values):
-        return jnp.where(from_below, pltpu.roll(values, 1, 0), pltpu.roll(values, ny - 1, 0))
-
-    def sources(x, e):
-        before = masked[0, x, e] + masked[1, x, e]
-        after = masked[0, x + 2, e] - masked[1, x + 2, e]
-        m, gy = masked[0, x + 1, e], masked[2, x + 1, e]
-        side_x = jnp.where(from_left, before, after)
-        side_y = jnp.where(
-            from_below, pltpu.roll(m + gy, 1, 0), pltpu.roll(m - gy, ny - 1, 0)
-        )
-        return side_x, side_y
-
-    def mask_of(x, e):
-        return jnp.where(cutb[x] > (first + e).astype(jnp.float32), 1.0, 0.0)
-
-    def level_step(x):
-        for e in range(ne):
-            vx, vy = speeds[e] * along, speeds[e] * across
-            ax, ay = jnp.abs(vx), jnp.abs(vy)
-            side_x, side_y = sources(x, e)
-            out_ref[0, x, e] = (
-                (keep[e] - ax - ay) * masked[0, x + 1, e]
-                - vx * masked[1, x + 1, e]
-                - vy * masked[2, x + 1, e]
-                + ax * side_x
-                + ay * inside * side_y
-            )
-
-    pl.loop(1, nx - 1, unroll=3)(level_step)
+    @pl.loop(1, n_mom)
+    def _(i):
+        target = (mom + i) % n_mom
+
+        @pl.when((target > 0) & (target < n_mom - 1))
+        def _():
+            density_copy(target, mom).start()
 
     @pl.when(has_right)
     def _():
@@ -250,8 +319,14 @@
     def _():
         to_right.wait_recv()
 
-    level_step(0)
-    level_step(nx - 1)
+    for edge in (0, nx - 1):
+        level_step(edge)
+        column = jnp.concatenate([totals[edge], jnp.zeros((nd - ny, nd), jnp.float32)], axis=0)
+        dens_send[edge] = lane_sums(column)[0:1] * (1.0 / (NE * NDIR))
+
+        @pl.when(mom != edge)
+        def _(edge=edge):
+            density_copy(edge, mom).start()
 
     for offset in offsets:
         there = (mom + offset >= 0) & (mom + offset < n_mom)
@@ -262,53 +337,16 @@
 
     def set_gains(c):
         gathered = moments[:, :, c * cells : (c + 1) * cells].reshape(depth, cells)
+        high, low = parts(gathered)
+        stacked = jnp.concatenate([high, low, high, jnp.zeros((8, cells), jnp.float32)], axis=0)
         gains[c] = lax.dot_general(
-            gathered,
+            stacked.astype(jnp.bfloat16),
             weights,
             (((0,), (0,)), ((), ())),
-            precision=lax.Precision.HIGHEST,
             preferred_element_type=jnp.float32,
         ).reshape(nx, ny, ne * nd)
 
-    set_gains(0)
-
-    @pl.loop(0, nx, unroll=4)
-    def _(x):
-        total = jnp.zeros((ny, nd), jnp.float32)
-        for e in range(ne):
-            raw0 = mask_of(x, e) * (out_ref[0, x, e] + gains[0, x, :, e * nd : (e + 1) * nd])
-            out_ref[0, x, e] = raw0
-            total = total + raw0
-        totals[x] = total
-
-    flat = lane_sums(totals[...].reshape(cells, nd))[0:1] * (1.0 / (NE * NDIR))
-    cell = lax.broadcasted_iota(jnp.int32, (nx, cells), 1)
-    column_of = lax.broadcasted_iota(jnp.int32, (nx, cells), 0)
-    spread_rows = jnp.where((cell // ny) == column_of, flat, 0.0)
-    source_y = lax.broadcasted_iota(jnp.int32, (cells, nd), 0) % ny
-    target_y = lax.broadcasted_iota(jnp.int32, (cells, nd), 1)
-    pick = jnp.where(source_y == target_y, 1.0, 0.0)
-    table = jnp.dot(
-        spread_rows, pick, precision=lax.Precision.HIGHEST, preferred_element_type=jnp.float32
-    )
-    for x in range(nx):
-        dens_send[x] = table[x : x + 1]
-
-    def density_copy(target, slot):
-        return pltpu.make_async_remote_copy(
-            src_ref=dens_send.at[target],
-            dst_ref=dens_recv.at[slot],
-            send_sem=den_send.at[target],
-            recv_sem=den_recv.at[slot],
-            device_id={"mom": target},
-            device_id_type=MESH,
-        )
-
-    @pl.loop(1, n_mom)
-    def _(i):
-        density_copy((mom + i) % n_mom, mom).start()
-
-    for c in range(1, comps):
+    for c in range(comps):
         set_gains(c)
 
     @pl.loop(0, nx, unroll=2)
@@ -334,8 +372,9 @@
             )
             raw1, raw2 = mask * raw1, mask * raw2
             spread = jnp.abs(raw1) + jnp.abs(raw2)
-            raw0 = out_ref[0, x, e]
+            raw0 = mask * (out_ref[0, x, e] + gains[0, x, :, e * nd : (e + 1) * nd])
             scaling = jnp.minimum(1.0, jnp.maximum(raw0, 0.0) / jnp.maximum(spread, FLOOR))
+            out_ref[0, x, e] = raw0
             out_ref[1, x, e] = scaling * raw1
             out_ref[2, x, e] = scaling * raw2
 

time: 31.4 us -> 29.3 us (0.933)
  the two profiles are of different devices: /device:TPU:1 before, /device:TPU:24 now
where the time goes in v4:
time: 29.3 us; the launch traced here: 29.1 us
  Pallas kernels  26.9 us (92%)
  local copies, waits for them, and re-layouts  1.53 us (5%)
  between operations  0.64 us (2%)
    pallas_call x1, Pallas kernels, on_device(): pl.pallas_call(functools.partial(kernel, n_space, n_mom), out_shape=(pltp...  26.9 us
    unnamed x2, local copies, waits for them, and re-layouts  1.53 us

profile of v4, /device:TPU:24, one launch (start us, length us, event | category | flops | bytes accessed | tf_op | source)
XLA Modules:
  0.0 29.1 jit_solution(13167485303214874828)
XLA Ops:
  0.6 26.9 %section.1 = (f32[3,32,3,8,128]{4,3,2,1,0:T(8,128)S(1)}, f32[1,8]{1,0:T(1,128)S(1)}) custom-call(f32[3,32,3,8,128]{4,3,2,1,0:T(8,128)} %bitcast.6, s32[8,32]{1,0:T(8,128)} %bitcast.7, s32[4]{0:T(128)} %shift_ref.1, f32[2,4]{1,0:T(2,128)} %rates_ref.1), custom_call_target="tpu_custom_call" | custom-call | tf_op jit(solution)/shard_map/section/pallas_call | solution.py:409
  27.6 1.0 %copy.8 = f32[3,32,8,3,128]{4,2,3,1,0:T(8,128)} copy(f32[3,32,8,3,128]{4,2,3,1,0:T(8,128)S(1)} %bitcast.4) | data formatting | bytes 2359296
  28.6 0.5 %copy.9 = f32[8]{0:T(128)} copy(f32[8]{0:T(128)S(1)} %bitcast.5) | data formatting | bytes 64

commit v5 on v4

--- a/solution.py
+++ b/solution.py
@@ -65,6 +65,8 @@
     totals,
     dens_send,
     dens_recv,
+    halo_out,
+    halo_in,
     load_sem,
     halo_send,
     halo_recv,
@@ -124,7 +126,13 @@
     for e in range(ne):
         rows = masked[:, 1 : nx + 1, e].reshape(comps * cells, nd)
         packed = jnp.where(row == e, lane_sums(rows) * (1.0 / NDIR), packed)
-    moments[reach] = packed
+    moments[reach] = packed[0:4]
+    upper = lax.broadcasted_iota(jnp.int32, (ny, nd), 1) >= nd // 2
+    for e in range(ne):
+        m, gx, gy = (masked[c, 1, e] for c in range(comps))
+        halo_out[0, e] = jnp.where(upper, pltpu.roll(gy, nd // 2, 1), m - gx)
+        m, gx, gy = (masked[c, nx, e] for c in range(comps))
+        halo_out[1, e] = jnp.where(upper, m + gx, pltpu.roll(gy, nd // 2, 1))
 
     along, across = cosines()
     depth = (2 * reach + 1) * 8
@@ -246,26 +254,26 @@
 
     @pl.when(jnp.logical_not(has_left))
     def _():
-        masked[:, 0] = jnp.zeros((comps, ne, ny, nd), jnp.float32)
+        halo_in[1] = jnp.zeros((ne, ny, nd), jnp.float32)
 
     @pl.when(jnp.logical_not(has_right))
     def _():
-        masked[:, nx + 1] = jnp.zeros((comps, ne, ny, nd), jnp.float32)
+        halo_in[0] = jnp.zeros((ne, ny, nd), jnp.float32)
 
     peers = n_mom - 1 + has_left.astype(jnp.int32) + has_right.astype(jnp.int32)
     pl.semaphore_wait(barrier, peers)
 
     to_left = pltpu.make_async_remote_copy(
-        src_ref=masked.at[:, 1],
-        dst_ref=masked.at[:, nx + 1],
+        src_ref=halo_out.at[0],
+        dst_ref=halo_in.at[0],
         send_sem=halo_send.at[0],
         recv_sem=halo_recv.at[0],
         device_id={"space": space - 1},
         device_id_type=MESH,
     )
     to_right = pltpu.make_async_remote_copy(
-        src_ref=masked.at[:, nx],
-        dst_ref=masked.at[:, 0],
+        src_ref=halo_out.at[1],
+        dst_ref=halo_in.at[1],
         send_sem=halo_send.at[1],
         recv_sem=halo_recv.at[1],
         device_id={"space": space + 1},
@@ -291,6 +299,14 @@
             device_id_type=MESH,
         )
 
+    @pl.loop(1, n_mom)
+    def _(i):
+        target = (mom + i) % n_mom
+
+        @pl.when((target > 0) & (target < n_mom - 1))
+        def _():
+            density_copy(target, mom).start()
+
     offsets = [o for o in range(-reach, reach + 1) if o != 0]
     for offset in offsets:
         there = (mom + offset >= 0) & (mom + offset < n_mom)
@@ -301,15 +317,7 @@
 
         @pl.when(jnp.logical_not(there))
         def _(offset=offset):
-            moments[reach + offset] = jnp.zeros((8, comps * cells), jnp.float32)
-
-    @pl.loop(1, n_mom)
-    def _(i):
-        target = (mom + i) % n_mom
-
-        @pl.when((target > 0) & (target < n_mom - 1))
-        def _():
-            density_copy(target, mom).start()
+            moments[reach + offset] = jnp.zeros((4, comps * cells), jnp.float32)
 
     @pl.when(has_right)
     def _():
@@ -318,6 +326,13 @@
     @pl.when(has_left)
     def _():
         to_right.wait_recv()
+
+    for side, place in ((1, 0), (0, nx + 1)):
+        for e in range(ne):
+            arrived = halo_in[side, e]
+            masked[0, place, e] = arrived
+            masked[1, place, e] = jnp.zeros((ny, nd), jnp.float32)
+            masked[2, place, e] = pltpu.roll(arrived, nd // 2, 1)
 
     for edge in (0, nx - 1):
         level_step(edge)
@@ -336,7 +351,8 @@
             moment_copy(-offset).wait_recv()
 
     def set_gains(c):
-        gathered = moments[:, :, c * cells : (c + 1) * cells].reshape(depth, cells)
+        gathered = moments[:, :, c * cells : (c + 1) * cells]
+        gathered = jnp.concatenate([gathered, jnp.zeros_like(gathered)], axis=1).reshape(depth, cells)
         high, low = parts(gathered)
         stacked = jnp.concatenate([high, low, high, jnp.zeros((8, cells), jnp.float32)], axis=0)
         gains[c] = lax.dot_general(
@@ -426,11 +442,13 @@
             pltpu.VMEM((comps, nx, ne, ny, nd), jnp.float32),
             pltpu.VMEM((comps, nx + 2, ne, ny, nd), jnp.float32),
             pltpu.VMEM((nx, ny, nd), jnp.float32),
-            pltpu.VMEM((2 * reach + 1, 8, comps * nx * ny), jnp.float32),
+            pltpu.VMEM((2 * reach + 1, 4, comps * nx * ny), jnp.float32),
             pltpu.VMEM((comps, nx, ny, ne * nd), jnp.float32),
             pltpu.VMEM((nx, ny, nd), jnp.float32),
             pltpu.VMEM((n_mom, 1, nd), jnp.float32),
             pltpu.VMEM((n_mom, 1, nd), jnp.float32),
+            pltpu.VMEM((2, ne, ny, nd), jnp.float32),
+            pltpu.VMEM((2, ne, ny, nd), jnp.float32),
             pltpu.SemaphoreType.DMA((comps,)),
             pltpu.SemaphoreType.DMA((2,)),
             pltpu.SemaphoreType.DMA((2,)),

time: 29.3 us -> 29 us (0.990)
  no operation moved by 1% of the time
where the time goes in v5:
time: 29 us; the launch traced here: 28.8 us
  Pallas kernels  26.7 us (92%)
  local copies, waits for them, and re-layouts  1.53 us (5%)
  between operations  0.64 us (2%)
    pallas_call x1, Pallas kernels, on_device(): pl.pallas_call(functools.partial(kernel, n_space, n_mom), out_shape=(pltp...  26.7 us
    unnamed x2, local copies, waits for them, and re-layouts  1.53 us

profile of v5, /device:TPU:24, one launch (start us, length us, event | category | flops | bytes accessed | tf_op | source)
XLA Modules:
  0.0 28.8 jit_solution(7904161220150654693)
XLA Ops:
  0.6 26.7 %section.1 = (f32[3,32,3,8,128]{4,3,2,1,0:T(8,128)S(1)}, f32[1,8]{1,0:T(1,128)S(1)}) custom-call(f32[3,32,3,8,128]{4,3,2,1,0:T(8,128)} %bitcast.6, s32[8,32]{1,0:T(8,128)} %bitcast.7, s32[4]{0:T(128)} %shift_ref.1, f32[2,4]{1,0:T(2,128)} %rates_ref.1), custom_call_target="tpu_custom_call" | custom-call | tf_op jit(solution)/shard_map/section/pallas_call | solution.py:425
  27.3 1.0 %copy.8 = f32[3,32,8,3,128]{4,2,3,1,0:T(8,128)} copy(f32[3,32,8,3,128]{4,2,3,1,0:T(8,128)S(1)} %bitcast.4) | data formatting | bytes 2359296
  28.3 0.5 %copy.9 = f32[8]{0:T(128)} copy(f32[8]{0:T(128)S(1)} %bitcast.5) | data formatting | bytes 64

commit v6 on v5

--- a/solution.py
+++ b/solution.py
@@ -334,10 +334,15 @@
             masked[1, place, e] = jnp.zeros((ny, nd), jnp.float32)
             masked[2, place, e] = pltpu.roll(arrived, nd // 2, 1)
 
-    for edge in (0, nx - 1):
+    edges = (0, nx - 1)
+    blank_rows = jnp.zeros((nd - ny, nd), jnp.float32)
+    for edge in edges:
         level_step(edge)
-        column = jnp.concatenate([totals[edge], jnp.zeros((nd - ny, nd), jnp.float32)], axis=0)
+    columns = [jnp.concatenate([totals[edge], blank_rows], axis=0) for edge in edges]
+    for edge, column in zip(edges, columns):
         dens_send[edge] = lane_sums(column)[0:1] * (1.0 / (NE * NDIR))
+
+    for edge in edges:
 
         @pl.when(mom != edge)
         def _(edge=edge):

time: 29 us -> 29 us (level)
  no operation moved by 1% of the time
where the time goes in v6:
time: 29 us; the launch traced here: 28.9 us
  Pallas kernels  26.7 us (92%)
  local copies, waits for them, and re-layouts  1.53 us (5%)
  between operations  0.64 us (2%)
    pallas_call x1, Pallas kernels, on_device(): pl.pallas_call(functools.partial(kernel, n_space, n_mom), out_shape=(pltp...  26.7 us
    unnamed x2, local copies, waits for them, and re-layouts  1.53 us

profile of v6, /device:TPU:24, one launch (start us, length us, event | category | flops | bytes accessed | tf_op | source)
XLA Modules:
  0.0 28.9 jit_solution(8892100027850128624)
XLA Ops:
  0.6 26.7 %section.1 = (f32[3,32,3,8,128]{4,3,2,1,0:T(8,128)S(1)}, f32[1,8]{1,0:T(1,128)S(1)}) custom-call(f32[3,32,3,8,128]{4,3,2,1,0:T(8,128)} %bitcast.6, s32[8,32]{1,0:T(8,128)} %bitcast.7, s32[4]{0:T(128)} %shift_ref.1, f32[2,4]{1,0:T(2,128)} %rates_ref.1), custom_call_target="tpu_custom_call" | custom-call | tf_op jit(solution)/shard_map/section/pallas_call | solution.py:430
  27.3 1.0 %copy.8 = f32[3,32,8,3,128]{4,2,3,1,0:T(8,128)} copy(f32[3,32,8,3,128]{4,2,3,1,0:T(8,128)S(1)} %bitcast.4) | data formatting | bytes 2359296
  28.3 0.5 %copy.9 = f32[8]{0:T(128)} copy(f32[8]{0:T(128)S(1)} %bitcast.5) | data formatting | bytes 64
